TPU v7x, 32 devices: a whole 2x2x4 slice. The times are simulated.
32 devices in a mesh: depth: 4 (over y, x), tile: 8 (over z, core).
Axes of the slice: x: 2, y: 2, z: 4, core: 2. Of those that a mesh axis runs over, the one named last changes fastest.
Arguments:
- density: bfloat16 [128, 512, 2048], P('depth', 'tile'), may hold values from 0 to 2
- depth_rank: int32 [4], replicated, may hold values from 0 to 3, as said below
- piece_home: int32 [64], P('tile'), may hold values from 0 to 63, as said below
Outputs:
- display: float32 [3, 4, 64, 4096], P(None, 'depth', 'tile')
Inputs may be any that keep to these rules, and one draw needn't show every extreme that they name: Either depth_rank[i] = i for every i, or depth_rank[i] = 3 - i for every i. `piece_home`: every value appears exactly once. A value h names slot h % 8 of the device h // 8 along tile. The number of the 8 entries of tile device s that name device o depends only on (o - s) mod 8, is at most 2, and equals 2 for some pair.
All inputs are finite; a program needn't handle non-finite values.
Results may differ from a plain program's by a relative error of at most 0.0003.
Values may be sent and summed in bfloat16 or wider, within the bound.
A program may use at most 128 MiB of HBM per device.

v0:
```python
import jax
import jax.numpy as jnp
from jax import lax
from jax.sharding import PartitionSpec as P

MOST = 2


EXTINCT = 0.5
LIGHT_Z = 0.6
LIGHT_Y = 0.48
LIGHT_X = 0.64
SHARPNESS = 6.0
BACKDROP = (0.08, 0.1, 0.14)


def with_halo(shard, sides, width):
    for axis, dim in sides:
        peers, length = (lax.axis_size(axis), shard.shape[dim])
        up = [(i, (i + 1) % peers) for i in range(peers - 1)]
        down = [(j, i) for i, j in up]
        last = lax.slice_in_dim(shard, length - width, length, axis=dim)
        leading = lax.slice_in_dim(shard, 0, width, axis=dim)
        before = lax.ppermute(last, axis, up)
        after = lax.ppermute(leading, axis, down)
        shard = jnp.concatenate([before, shard, after], axis=dim)
    return shard


def lighting(padded):
    center = padded[1:-1, 1:-1, :]
    grad_z = 0.5 * (padded[2:, 1:-1, :] - padded[:-2, 1:-1, :])
    grad_y = 0.5 * (padded[1:-1, 2:, :] - padded[1:-1, :-2, :])
    padded_x = jnp.pad(center, ((0, 0), (0, 0), (1, 1)))
    grad_x = 0.5 * (padded_x[:, :, 2:] - padded_x[:, :, :-2])
    facing = LIGHT_Z * grad_z + LIGHT_Y * grad_y + LIGHT_X * grad_x
    shading = 0.35 + 0.65 * (0.5 + 0.5 * jnp.tanh(SHARPNESS * facing))
    return (center, shading)


def emission(center):
    logged = jnp.log(center + 0.01)
    return (
        jax.nn.sigmoid(logged + 3.0),
        0.5 + 0.5 * jnp.cos(1.7 * logged),
        jax.nn.sigmoid(-(logged + 2.5)),
    )


def on_device(density, depth_rank, piece_home):
    depth_cells, row_count, columns = density.shape
    padded = with_halo(density, (("depth", 0), ("tile", 1)), 1)
    center, shading = lighting(padded.astype(jnp.float32))
    optical = EXTINCT * center
    ascend = depth_rank[0] == 0
    forward = lax.cumsum(optical, 0) - optical
    backward = lax.cumsum(optical, 0, reverse=True) - optical
    before = jnp.where(ascend, forward, backward)
    weight = jnp.exp(-before) * -jnp.expm1(-optical) * shading
    colors = emission(center)
    radiance = jnp.stack([jnp.sum(weight * channel, axis=0) for channel in colors])
    through = jnp.exp(-jnp.sum(optical, axis=0))
    partial_image = jnp.concatenate([radiance, through[None]], 0)
    depth_count = lax.axis_size("depth")
    quarter = row_count * columns // depth_count
    layered = partial_image.reshape(4, depth_count, quarter)
    gathered = lax.all_to_all(layered, "depth", split_axis=1, concat_axis=1, tiled=True)
    color_acc = gathered[:3, 0]
    trans_acc = gathered[3:4, 0]
    for member in range(1, depth_count):
        color_new = gathered[:3, member]
        trans_new = gathered[3:4, member]
        color_acc = jnp.where(
            ascend, color_acc + trans_acc * color_new, color_new + trans_new * color_acc
        )
        trans_acc = trans_acc * trans_new
    merged = jnp.concatenate([color_acc, trans_acc], 0)
    backdrop = jnp.array(BACKDROP, jnp.float32)[:, None]
    finished = merged[:3] + merged[3:4] * backdrop
    tile_count = lax.axis_size("tile")
    piece_len = quarter // tile_count
    pieces = finished.reshape(3, tile_count, piece_len)
    owners = piece_home // tile_count
    slots = piece_home % tile_count
    order_index = jnp.arange(tile_count)
    shared = owners[:, None] == owners[None, :]
    earlier_count = jnp.sum(
        (shared & (order_index[None, :] < order_index[:, None])).astype(jnp.int32), axis=1
    )
    target = owners * MOST + earlier_count
    outbox_index = jnp.arange(tile_count * MOST)
    routing = (outbox_index[:, None] == target[None, :]).astype(jnp.float32)
    outbox = jnp.einsum("sp,cpr->scr", routing, pieces, precision=lax.Precision.HIGHEST)
    labels = (
        jnp.dot(routing, (slots + 1).astype(jnp.float32), precision=lax.Precision.HIGHEST) - 1.0
    )
    outbox = outbox.reshape(tile_count, MOST, 3, piece_len)
    labels = labels.reshape(tile_count, MOST)
    arrived, arrived_labels = (
        lax.all_to_all(outbox, "tile", split_axis=0, concat_axis=0, tiled=True),
        lax.all_to_all(labels, "tile", split_axis=0, concat_axis=0, tiled=True),
    )
    flat_pieces = arrived.reshape(tile_count * MOST, 3, piece_len)
    flat_labels = arrived_labels.reshape(-1).astype(jnp.int32)
    placing = (order_index[:, None] == flat_labels[None, :]).astype(jnp.float32)
    display = jnp.einsum("qs,scr->cqr", placing, flat_pieces, precision=lax.Precision.HIGHEST)
    return display[:, None]


def solution(mesh):
    in_specs = (P("depth", "tile", None), P(), P("tile"))
    out_specs = P(None, "depth", "tile", None)
    return jax.shard_map(
        on_device, mesh=mesh, in_specs=in_specs, out_specs=out_specs, check_vma=False
    )
```

profile of v0, /device:TPU:0, one launch (start us, length us, event | category | flops | bytes accessed | tf_op | source)
XLA Modules:
  0.0 235.4 jit_solution(15381328334654492131)
XLA Ops:
  0.0 0.0 copy-start.1
  0.0 1.1 fusion.48
  1.1 4.9 %collective-permute-start = (bf16[1,64,2048]{2,1,0:T(8,128)(2,1)S(1)}, bf16[1,64,2048]{2,1,0:T(8,128)(2,1)S(1)}, u32[]{:S(2)}, u32[]{:S(2)}) collective-permute-start(bf16[1,64,2048]{2,1,0:T(8,128)(2,1)S(1)} %get-tuple-element.15), channel_id=1, source_target_pairs={{0,8},{8,16},{16,24},{1,9},{9,17},{17,25},{2,10},{10,18},{18,26},{... | collective-permute-start | bytes 786440 | tf_op jit(solution)/shard_map/ppermute | solution.py:24
  6.0 1.3 collective-permute-start.1
  7.3 4.2 %collective-permute-done = bf16[1,64,2048]{2,1,0:T(8,128)(2,1)S(1)} collective-permute-done((bf16[1,64,2048]{2,1,0:T(8,128)(2,1)S(1)}, bf16[1,64,2048]{2,1,0:T(8,128)(2,1)S(1)}, u32[]{:S(2)}, u32[]{:S(2)}) %collective-permute-start) | collective-permute-done | bytes 262176 | tf_op jit(solution)/shard_map/ppermute | solution.py:24
  11.5 0.7 constant_dynamic-update-slice_fusion.2
  12.2 8.3 %constant_dynamic-update-slice_fusion.1 = bf16[34,64,2048]{2,1,0:T(8,128)(2,1)} fusion(bf16[34,64,2048]{2,1,0:T(8,128)(2,1)} %constant_dynamic-update-slice_fusion.2, bf16[32,64,2048]{2,1,0:T(8,128)(2,1)} %param.4), kind=kLoop, calls=%fused_computation.39 | loop fusion | bytes 16777216
  20.5 0.0 collective-permute-done.1
  20.5 0.7 constant_dynamic-update-slice_fusion
  21.2 2.0 fusion.47
  23.2 1.3 collective-permute-start.2
  24.6 1.3 collective-permute-start.3
  25.9 0.0 copy-done.1
  25.9 0.0 collective-permute-done.2
  25.9 3.9 %collective-permute-done.3 = bf16[34,1,2048]{2,1,0:T(2,128)(2,1)S(1)} collective-permute-done((bf16[34,1,2048]{2,1,0:T(2,128)(2,1)S(1)}, bf16[34,1,2048]{2,1,0:T(2,128)(2,1)S(1)}, u32[]{:S(2)}, u32[]{:S(2)}) %collective-permute-start.3) | collective-permute-done | bytes 139296 | tf_op jit(solution)/shard_map/ppermute | solution.py:25
  29.8 6.7 %maximum_convert_fusion = f32[34,66,2048]{2,1,0:T(8,128)S(1)} fusion(bf16[34,1,2048]{2,1,0:T(2,128)(2,1)S(1)} %collective-permute-done.3, bf16[34,64,2048]{2,1,0:T(8,128)(2,1)} %constant_dynamic-update-slice_fusion, bf16[34,1,2048]{2,1,0:T(2,128)(2,1)S(1)} %collective-permute-done.2), kind=kLoop, calls=%fused_computation.26 | loop fusion | flops 27574272 | bytes 27574272 | tf_op jit(solution)/shard_map/convert_element_type | solution.py:53
  36.5 7.0 %fusion.15 = f32[32,64,2048]{2,1,0:T(8,128)} fusion(f32[34,66,2048]{2,1,0:T(8,128)S(1)} %maximum_convert_fusion), kind=kOutput, calls=%fused_computation.24 | output fusion | flops 134217728 | bytes 33554432 | tf_op jit(solution)/shard_map/on_device/reduce_window_sum | solution.py:56
  43.5 6.2 %slice.82 = f32[32,64,2048]{2,1,0:T(8,128)} slice(f32[34,66,2048]{2,1,0:T(8,128)S(1)} %maximum_convert_fusion), slice={[1:33], [1:65], [0:2048]} | slice | bytes 33554432 | tf_op jit(solution)/shard_map/slice | solution.py:31
  49.7 0.0 copy-start.2
  49.7 0.0 copy-start
  49.7 107.3 %multiply_reduce_fusion.2 = (f32[64,2048]{1,0:T(8,128)}, f32[64,2048]{1,0:T(8,128)S(1)}, f32[64,2048]{1,0:T(8,128)}, f32[64,2048]{1,0:T(8,128)S(1)}) fusion(f32[34,66,2048]{2,1,0:T(8,128)S(1)} %maximum_convert_fusion, f32[32,64,2048]{2,1,0:T(8,128)} %slice.82, f32[32,64,2048]{2,1,0:T(8,128)} %fusion.15, pred[]{:T(512)} %bitcast.2), kind=kOutput, calls=%fused_computation.19 | output fusion | flops 305659904 | bytes 136314880 | tf_op jit(solution)/shard_map/on_device/reduce_window_sum | solution.py:57
  157.0 0.1 negate_exponential_fusion
  157.1 0.6 exp.27
  157.8 1.7 concatenate.18
  159.4 1.7 concatenate.19
  161.1 0.6 concatenate.20
  161.7 3.3 %pad_maximum_fusion = f32[4,4,32768]{2,0,1:T(4,128)} fusion(f32[1,4,32768]{2,0,1:T(1,128)S(1)} %exp.27, f32[1,4,32768]{2,0,1:T(1,128)S(1)} %concatenate.20, f32[1,4,32768]{2,0,1:T(1,128)S(1)} %concatenate.19, f32[1,4,32768]{2,0,1:T(1,128)S(1)} %concatenate.18), kind=kLoop, calls=%fused_computation.30 | loop fusion | flops 1572864 | bytes 4194304 | tf_op jit(solution)/shard_map/concatenate | solution.py:63
  165.0 5.8 %all-to-all-start = ((f32[4,4,32768]{2,0,1:T(4,128)}), f32[4,4,32768]{2,0,1:T(4,128)S(1)}, u32[]{:S(2)}, u32[]{:S(2)}) async-start(f32[4,4,32768]{2,0,1:T(4,128)} %pad_maximum_fusion), calls=%async_computation | async-start | bytes 4194304 | tf_op jit(solution)/shard_map/all_to_all | solution.py:67
  170.8 0.0 copy-done.2
  170.9 0.2 convert_reduce_fusion.1
  171.1 0.1 fusion.19
  171.2 0.7 all_to_all.14
  171.9 24.8 %all-to-all-done = f32[4,4,32768]{2,0,1:T(4,128)S(1)} async-done(((f32[4,4,32768]{2,0,1:T(4,128)}), f32[4,4,32768]{2,0,1:T(4,128)S(1)}, u32[]{:S(2)}, u32[]{:S(2)}) %all-to-all-start) | async-done | bytes 2097184 | tf_op jit(solution)/shard_map/all_to_all | solution.py:67
  196.6 7.1 %all-to-all-start.2 = ((f32[8,1,2]{2,1,0:T(1,128)}), f32[8,1,2]{2,1,0:T(1,128)S(1)}, u32[]{:S(2)}, u32[]{:S(2)}) async-start(f32[8,1,2]{2,1,0:T(1,128)} %bitcast.9), calls=%async_computation.2 | async-start | bytes 8192 | tf_op jit(solution)/shard_map/all_to_all | solution.py:101
  203.7 0.5 fusion.49
  204.3 0.0 copy-done
  204.3 0.7 multiply_add_fusion
  205.0 0.6 fusion.20
  205.6 1.5 copy.16
  207.1 2.1 all-to-all-done.2
  209.2 3.5 %all-to-all-start.1 = ((f32[8,2,3,4096]{3,1,2,0:T(2,128)}), f32[8,2,3,4096]{3,1,2,0:T(2,128)S(1)}, u32[]{:S(2)}, u32[]{:S(2)}) async-start(f32[8,2,3,4096]{3,1,2,0:T(2,128)} %copy.16), calls=%async_computation.1 | async-start | bytes 1572864 | tf_op jit(solution)/shard_map/all_to_all | solution.py:100
  212.8 0.1 convert_element_type.27
  212.9 20.8 %all-to-all-done.1 = f32[8,2,3,4096]{3,1,2,0:T(2,128)S(1)} async-done(((f32[8,2,3,4096]{3,1,2,0:T(2,128)}), f32[8,2,3,4096]{3,1,2,0:T(2,128)S(1)}, u32[]{:S(2)}, u32[]{:S(2)}) %all-to-all-start.1) | async-done | bytes 786464 | tf_op jit(solution)/shard_map/all_to_all | solution.py:100
  233.6 0.1 copy.17
  233.7 0.5 reshape.209
  234.3 1.1 convolution_bitcast_fusion
  (5 shorter events, 0.1 us)
Async XLA Ops:
  0.0 25.9 %copy-start.1 = (s32[4]{0:T(128)S(1)}, s32[4]{0:T(128)}, u32[]{:S(2)}) copy-start(s32[4]{0:T(128)} %param.5) | copy-start | bytes 52
  1.1 10.4 %collective-permute-start = (bf16[1,64,2048]{2,1,0:T(8,128)(2,1)S(1)}, bf16[1,64,2048]{2,1,0:T(8,128)(2,1)S(1)}, u32[]{:S(2)}, u32[]{:S(2)}) collective-permute-start(bf16[1,64,2048]{2,1,0:T(8,128)(2,1)S(1)} %get-tuple-element.15), channel_id=1, source_target_pairs={{0,8},{8,16},{16,24},{1,9},{9,17},{17,25},{2,10},{10,18},{18,26},{... | collective-permute-start | bytes 786440 | tf_op jit(solution)/shard_map/ppermute | solution.py:24
  6.0 14.5 %collective-permute-start.1 = (bf16[1,64,2048]{2,1,0:T(8,128)(2,1)S(1)}, bf16[1,64,2048]{2,1,0:T(8,128)(2,1)S(1)}, u32[]{:S(2)}, u32[]{:S(2)}) collective-permute-start(bf16[1,64,2048]{2,1,0:T(8,128)(2,1)S(1)} %get-tuple-element.14), channel_id=1, source_target_pairs={{8,0},{16,8},{24,16},{9,1},{17,9},{25,17},{10,2},{18,10},{26,18},{... | collective-permute-start | bytes 786440 | tf_op jit(solution)/shard_map/ppermute | solution.py:25
  23.2 2.7 %collective-permute-start.2 = (bf16[34,1,2048]{2,1,0:T(2,128)(2,1)S(1)}, bf16[34,1,2048]{2,1,0:T(2,128)(2,1)S(1)}, u32[]{:S(2)}, u32[]{:S(2)}) collective-permute-start(bf16[34,1,2048]{2,1,0:T(2,128)(2,1)S(1)} %get-tuple-element.12), channel_id=1, source_target_pairs={{0,1},{1,2},{2,3},{3,4},{4,5},{5,6},{6,7},{8,9},{9,10},{10,11},{11... | collective-permute-start | bytes 417800 | tf_op jit(solution)/shard_map/ppermute | solution.py:24
  24.6 5.2 %collective-permute-start.3 = (bf16[34,1,2048]{2,1,0:T(2,128)(2,1)S(1)}, bf16[34,1,2048]{2,1,0:T(2,128)(2,1)S(1)}, u32[]{:S(2)}, u32[]{:S(2)}) collective-permute-start(bf16[34,1,2048]{2,1,0:T(2,128)(2,1)S(1)} %get-tuple-element.13), channel_id=1, source_target_pairs={{1,0},{2,1},{3,2},{4,3},{5,4},{6,5},{7,6},{9,8},{10,9},{11,10},{12... | collective-permute-start | bytes 417800 | tf_op jit(solution)/shard_map/ppermute | solution.py:25
  49.7 121.1 %copy-start.2 = (s32[8]{0:T(128)S(1)}, s32[8]{0:T(128)}, u32[]{:S(2)}) copy-start(s32[8]{0:T(128)} %param.6) | copy-start | bytes 100
  49.7 154.6 %copy-start = (f32[3]{0:T(128)S(1)}, f32[3]{0:T(128)}, u32[]{:S(2)}) copy-start(f32[3]{0:T(128)} %constant.74.clone) | copy-start | bytes 40
  165.0 31.6 %all-to-all-start = ((f32[4,4,32768]{2,0,1:T(4,128)}), f32[4,4,32768]{2,0,1:T(4,128)S(1)}, u32[]{:S(2)}, u32[]{:S(2)}) async-start(f32[4,4,32768]{2,0,1:T(4,128)} %pad_maximum_fusion), calls=%async_computation | async-start | bytes 4194304 | tf_op jit(solution)/shard_map/all_to_all | solution.py:67
  196.6 12.6 %all-to-all-start.2 = ((f32[8,1,2]{2,1,0:T(1,128)}), f32[8,1,2]{2,1,0:T(1,128)S(1)}, u32[]{:S(2)}, u32[]{:S(2)}) async-start(f32[8,1,2]{2,1,0:T(1,128)} %bitcast.9), calls=%async_computation.2 | async-start | bytes 8192 | tf_op jit(solution)/shard_map/all_to_all | solution.py:101
  209.2 24.4 %all-to-all-start.1 = ((f32[8,2,3,4096]{3,1,2,0:T(2,128)}), f32[8,2,3,4096]{3,1,2,0:T(2,128)S(1)}, u32[]{:S(2)}, u32[]{:S(2)}) async-start(f32[8,2,3,4096]{3,1,2,0:T(2,128)} %copy.16), calls=%async_computation.1 | async-start | bytes 1572864 | tf_op jit(solution)/shard_map/all_to_all | solution.py:100
where the time goes:
time: 236 us; the launch traced here: 235 us
  other arithmetic  125 us (53%)
  waiting for transfers between devices  55.8 us (24%)
  local copies, waits for them, and re-layouts  27 us (11%)
  starting transfers between devices  25.2 us (11%)
    another operation x1, other arithmetic, on_device(): backward = lax.cumsum(optical, 0, reverse=True) - optical  107 us
    all_to_all x1, waiting for transfers between devices, on_device(): lax.all_to_all(layered, 'depth', split_axis=1, concat_axis=1, tiled=True)  24.8 us
    all_to_all x1, waiting for transfers between devices, on_device(): lax.all_to_all(outbox, 'tile', split_axis=0, concat_axis=0, tiled=True)  20.8 us
    unnamed x8, local copies, waits for them, and re-layouts  8.98 us
    all_to_all x1, starting transfers between devices, on_device(): lax.all_to_all(labels, 'tile', split_axis=0, concat_axis=0, tiled=True)  7.07 us
    another operation x1, other arithmetic, on_device(): forward = lax.cumsum(optical, 0) - optical  6.97 us
    convert_element_type x1, other arithmetic, on_device(): center, shading = lighting(padded.astype(jnp.float32))  6.72 us
    slice x1, local copies, waits for them, and re-layouts, lighting(): center = padded[1:-1, 1:-1, :]  6.21 us
  transfers between devices with their start and end apart: 7, of which 5 were waited for; matrix products, arithmetic and copies ran while one was open for 5% of the time, Pallas kernels for 0%

commit v1 on v0

v1 whole, which is shorter than its diff:
```python
import functools
import math
import jax
import jax.numpy as jnp
import numpy as np
from jax import lax
from jax.experimental import pallas as pl
from jax.experimental.pallas import tpu as pltpu
from jax.sharding import PartitionSpec as P

MOST = 2

EXTINCT = 0.5
LIGHT_Z = 0.6
LIGHT_Y = 0.48
LIGHT_X = 0.64
SHARPNESS = 6.0
BACKDROP = (0.08, 0.1, 0.14)

HALO = 16
PAD = 128
CB = 256
RB = 16
SIG_A = math.exp(-3.0)
SIG_B = math.exp(-2.5)
COS = (1.9999999935320312, -0.9999997751464547, 0.08333208188264607,
       -0.002775337047259153, 4.7654375196060637e-05)


def stencils(rows):
    span = rows + HALO
    wy, wz = LIGHT_Y / LIGHT_X, LIGHT_Z / LIGHT_X
    left = np.zeros((rows, 3 * span), np.float32)
    for r in range(rows):
        left[r, r] = -wz
        left[r, 2 * span + r] = wz
        left[r, span + (r + 1 if r < rows - 1 else rows)] = wy
        left[r, span + (r - 1 if r > 0 else rows + 1)] = -wy
    right = np.zeros((CB + 2 * PAD, CB), np.float32)
    for c in range(CB):
        right[c + PAD + 1, c] = 1.0
        right[c + PAD - 1, c] = -1.0
    return jnp.asarray(left, jnp.bfloat16), jnp.asarray(right, jnp.bfloat16)


def make_facing(d, g, left, right, cells, rows, zc):
    span = rows + HALO

    def facing(block, slot, chunk):
        z0 = chunk * zc
        c0 = pl.multiple_of(block * CB, CB)
        wide = d[pl.ds(z0 + 1, zc), :, pl.ds(c0, CB + 2 * PAD)]
        dx = jnp.dot(wide.reshape(zc * span, CB + 2 * PAD), right[...],
                     preferred_element_type=jnp.float32)
        c1 = pl.multiple_of(block * CB + PAD, PAD)
        for i in range(zc):
            tall = d[pl.ds(z0 + i, 3), :, pl.ds(c1, CB)].reshape(3 * span, CB)
            dyz = jnp.dot(left[...], tall, preferred_element_type=jnp.float32)
            g[slot, z0 + i] = dyz + dx[i * span:i * span + rows]

    return facing


def march(d, g, state, ascend, block, slot, rb, half, halves, cells):
    steps = cells // halves
    first = half == 0
    shape = (RB, CB)
    trans = jnp.where(first, 1.0, state[0])
    total, m0, m1, wave = (jnp.where(first, 0.0, state[i]) for i in range(1, 5))
    r0 = pl.multiple_of(rb * RB, RB)
    c1 = pl.multiple_of(block * CB + PAD, PAD)
    bias = (0.35 + 0.65 * 0.5) / (0.65 * 0.5)
    for i in range(steps):
        k = half * steps + i
        z = jnp.where(ascend, k, cells - 1 - k)
        dens = d[z + 1, pl.ds(r0, RB), pl.ds(c1, CB)].astype(jnp.float32)
        face = g[slot, z, pl.ds(r0, RB), :]
        shade = jnp.tanh(face * (0.5 * SHARPNESS * LIGHT_X)) + bias
        after = trans * jnp.exp2(dens * (-EXTINCT * math.log2(math.e)))
        ws = (trans - after) * shade
        trans = after
        u = dens + 0.01
        wr = ws / ((u + SIG_A) * (u + SIG_B))
        x = jnp.log(u) * (1.7 / 4) + math.pi / 4
        s = x * x
        c = COS[4] * s + COS[3]
        c = c * s + COS[2]
        c = c * s + COS[1]
        c = c * s + COS[0]
        v = c * c - 2.0
        total = total + ws
        m0 = m0 + wr
        m1 = m1 + wr * u
        wave = wave + ws * (v * v)
    for i, val in enumerate((trans, total, m0, m1, wave)):
        state[i] = val
    scale = 0.65 * 0.5
    return (
        scale * (total - SIG_A * (m1 + SIG_B * m0)),
        scale * (total - 0.25 * wave),
        scale * SIG_B * (m1 + SIG_A * m0),
        trans,
    )


def brick_kernel(rank, dens, zlo, zhi, yh, left, right, out, d, g, state, sems):
    cells, rows, cols = dens.shape
    nb, bands, halves = cols // CB, rows // RB, 2
    its = bands * halves
    zc = cells // its
    ascend = rank[0] == 0

    def copies(block):
        src = pl.ds(pl.multiple_of(block * CB, CB), CB)
        dst = pl.ds(pl.multiple_of(block * CB + PAD, PAD), CB)
        mk = pltpu.make_async_copy
        return (
            mk(dens.at[:, :, src], d.at[pl.ds(1, cells), pl.ds(0, rows), dst], sems.at[0, block]),
            mk(yh.at[:, :, src], d.at[pl.ds(1, cells), pl.ds(rows, HALO), dst], sems.at[1, block]),
            mk(zlo.at[:, src], d.at[0, pl.ds(0, rows), dst], sems.at[2, block]),
            mk(zhi.at[:, src], d.at[cells + 1, pl.ds(0, rows), dst], sems.at[3, block]),
        )

    @pl.loop(0, nb)
    def _(b):
        for cp in copies(b):
            cp.start()

    side = jnp.zeros((cells + 2, rows + HALO, PAD), d.dtype)
    d[:, :, :PAD] = side
    d[:, :, cols + PAD:] = side
    edge = jnp.zeros((HALO, cols), d.dtype)
    d[0, rows:, PAD:cols + PAD] = edge
    d[cells + 1, rows:, PAD:cols + PAD] = edge
    facing = make_facing(d, g, left, right, cells, rows, zc)

    def arrive(b):
        for cp in copies(b):
            cp.wait()

    arrive(0)
    arrive(1)

    @pl.loop(0, its)
    def _(it):
        facing(0, 0, it)

    @pl.loop(0, nb)
    def _(b):
        @pl.when(b + 2 < nb)
        def _():
            arrive(b + 2)

        slot = lax.rem(b, 2)
        ahead = jnp.minimum(b + 1, nb - 1)

        @pl.loop(0, its)
        def _(it):
            facing(ahead, 1 - slot, it)
            rb = it // halves
            vals = march(d, g, state, ascend, b, slot, rb, lax.rem(it, halves), halves, cells)
            for ch, val in enumerate(vals):
                out[ch, pl.ds(pl.multiple_of(rb * RB, RB), RB), pl.ds(pl.multiple_of(b * CB, CB), CB)] = val


def partial_image_of(density, depth_rank, zlo, zhi, yh):
    cells, rows, cols = density.shape
    left, right = stencils(rows)
    anyspec = pl.BlockSpec(memory_space=pl.ANY)
    vmem = pl.BlockSpec(memory_space=pltpu.VMEM)
    return pl.pallas_call(
        brick_kernel,
        out_shape=jax.ShapeDtypeStruct((4, rows, cols), jnp.float32),
        in_specs=[pl.BlockSpec(memory_space=pltpu.SMEM)] + [anyspec] * 4 + [vmem] * 2,
        out_specs=vmem,
        scratch_shapes=[
            pltpu.VMEM((cells + 2, rows + HALO, cols + 2 * PAD), jnp.bfloat16),
            pltpu.VMEM((2, cells, rows, CB), jnp.float32),
            pltpu.VMEM((5, RB, CB), jnp.float32),
            pltpu.SemaphoreType.DMA((4, cols // CB)),
        ],
        compiler_params=pltpu.CompilerParams(vmem_limit_bytes=48 * 1024 * 1024),
    )(depth_rank, density, zlo, zhi, yh, left, right)


def edges(density):
    cells, rows, cols = density.shape

    def move(x, axis, step):
        n = lax.axis_size(axis)
        return lax.ppermute(x, axis, [(i, i + step) for i in range(n) if 0 <= i + step < n])

    zlo = move(density[cells - 1], "depth", 1)
    zhi = move(density[0], "depth", -1)
    ylo = move(density[:, rows - 1], "tile", 1)
    yhi = move(density[:, 0], "tile", -1)
    yh = jnp.concatenate(
        [yhi[:, None], ylo[:, None], jnp.zeros((cells, HALO - 2, cols), density.dtype)], axis=1
    )
    return zlo, zhi, yh


def on_device(density, depth_rank, piece_home):
    depth_cells, row_count, columns = density.shape
    ascend = depth_rank[0] == 0
    partial_image = partial_image_of(density, depth_rank, *edges(density))
    depth_count = lax.axis_size("depth")
    quarter = row_count * columns // depth_count
    layered = partial_image.reshape(4, depth_count, row_count // depth_count, columns)
    gathered = lax.all_to_all(layered, "depth", split_axis=1, concat_axis=1, tiled=True)
    color_acc = gathered[:3, 0]
    trans_acc = gathered[3:4, 0]
    for member in range(1, depth_count):
        color_new = gathered[:3, member]
        trans_new = gathered[3:4, member]
        color_acc = jnp.where(
            ascend, color_acc + trans_acc * color_new, color_new + trans_new * color_acc
        )
        trans_acc = trans_acc * trans_new
    merged = jnp.concatenate([color_acc, trans_acc], 0)
    backdrop = jnp.array(BACKDROP, jnp.float32)[:, None]
    merged = merged.reshape(4, quarter)
    finished = merged[:3] + merged[3:4] * backdrop
    tile_count = lax.axis_size("tile")
    piece_len = quarter // tile_count
    pieces = finished.reshape(3, tile_count, piece_len)
    owners = piece_home // tile_count
    slots = piece_home % tile_count
    order_index = jnp.arange(tile_count)
    shared = owners[:, None] == owners[None, :]
    earlier_count = jnp.sum(
        (shared & (order_index[None, :] < order_index[:, None])).astype(jnp.int32), axis=1
    )
    target = owners * MOST + earlier_count
    outbox_index = jnp.arange(tile_count * MOST)
    routing = (outbox_index[:, None] == target[None, :]).astype(jnp.float32)
    outbox = jnp.einsum("sp,cpr->scr", routing, pieces, precision=lax.Precision.HIGHEST)
    labels = (
        jnp.dot(routing, (slots + 1).astype(jnp.float32), precision=lax.Precision.HIGHEST) - 1.0
    )
    outbox = outbox.reshape(tile_count, MOST, 3, piece_len)
    labels = labels.reshape(tile_count, MOST)
    arrived, arrived_labels = (
        lax.all_to_all(outbox, "tile", split_axis=0, concat_axis=0, tiled=True),
        lax.all_to_all(labels, "tile", split_axis=0, concat_axis=0, tiled=True),
    )
    flat_pieces = arrived.reshape(tile_count * MOST, 3, piece_len)
    flat_labels = arrived_labels.reshape(-1).astype(jnp.int32)
    placing = (order_index[:, None] == flat_labels[None, :]).astype(jnp.float32)
    display = jnp.einsum("qs,scr->cqr", placing, flat_pieces, precision=lax.Precision.HIGHEST)
    return display[:, None]


def solution(mesh):
    in_specs = (P("depth", "tile", None), P(), P("tile"))
    out_specs = P(None, "depth", "tile", None)
    return jax.shard_map(
        on_device, mesh=mesh, in_specs=in_specs, out_specs=out_specs, check_vma=False
    )
```

time: 236 us -> 140 us (0.59)
  other arithmetic: 125 us -> 1.19 us
  Pallas kernels: 0 us -> 43.8 us
  local copies, waits for them, and re-layouts: 27 us -> 12.1 us
    another operation x2 -> x0, other arithmetic: 114 us -> none  [the longest x1 107 us: on_device(): backward = lax.cumsum(optical, 0, reverse=True) - optical]
    pallas_call x0 -> x1, Pallas kernels: none -> 43.8 us  [partial_image_of(): pl.pallas_call(brick_kernel, out_shape=jax.ShapeDtypeStruct((4, rows, col...]
    unnamed x8 -> x16, local copies, waits for them, and re-layouts: 8.98 us -> 0.2 us
    convert_element_type x1 -> x0, other arithmetic: 6.72 us -> none  [on_device(): center, shading = lighting(padded.astype(jnp.float32))]
    slice x3 -> x2, local copies, waits for them, and re-layouts: 9.32 us -> 2.86 us  [the longest x1 1.97 us: edges(): yhi = move(density[:, 0], 'tile', -1)]
    concatenate x4 -> x1, local copies, waits for them, and re-layouts: 4.66 us -> 0.08 us  [edges(): jnp.concatenate([yhi[:, None], ylo[:, None], jnp.zeros((cells, HALO - 2,...]
    all_to_all x1, starting transfers between devices: 7.07 us -> 3.85 us  [on_device(): lax.all_to_all(labels, 'tile', split_axis=0, concat_axis=0, tiled=True)]
    ppermute x4, waiting for transfers between devices: 8.13 us -> 11.3 us  [move(): lax.ppermute(x, axis, [(i, i + step) for i in range(n) if 0 <= i + step <...]
  transfers between devices with their start and end apart: 7 -> 7, of which waited for: 5 -> 4; matrix products, arithmetic and copies ran while one was open for 5% -> 7% of each run, Pallas kernels for 0% -> 0%
where the time goes in v1:
time: 140 us; the launch traced here: 139 us
  waiting for transfers between devices  56.4 us (40%)
  Pallas kernels  43.8 us (31%)
  starting transfers between devices  23.3 us (17%)
  local copies, waits for them, and re-layouts  12.1 us (9%)
  matrix products  1.98 us (1%)
    pallas_call x1, Pallas kernels, partial_image_of(): pl.pallas_call(brick_kernel, out_shape=jax.ShapeDtypeStruct((4, rows, col...  43.8 us
    all_to_all x1, waiting for transfers between devices, on_device(): lax.all_to_all(layered, 'depth', split_axis=1, concat_axis=1, tiled=True)  24.3 us
    all_to_all x1, waiting for transfers between devices, on_device(): lax.all_to_all(outbox, 'tile', split_axis=0, concat_axis=0, tiled=True)  20.8 us
    ppermute x4, waiting for transfers between devices, move(): lax.ppermute(x, axis, [(i, i + step) for i in range(n) if 0 <= i + step <...  11.3 us
    ppermute x4, starting transfers between devices, move(): lax.ppermute(x, axis, [(i, i + step) for i in range(n) if 0 <= i + step <...  10.6 us
    all_to_all x1, starting transfers between devices, on_device(): lax.all_to_all(outbox, 'tile', split_axis=0, concat_axis=0, tiled=True)  5.1 us
    all_to_all x1, starting transfers between devices, on_device(): lax.all_to_all(labels, 'tile', split_axis=0, concat_axis=0, tiled=True)  3.85 us
    all_to_all x1, starting transfers between devices, on_device(): lax.all_to_all(layered, 'depth', split_axis=1, concat_axis=1, tiled=True)  3.74 us
  transfers between devices with their start and end apart: 7, of which 4 were waited for; matrix products, arithmetic and copies ran while one was open for 7% of the time, Pallas kernels for 0%

profile of v1, /device:TPU:0, one launch (start us, length us, event | category | flops | bytes accessed | tf_op | source)
XLA Modules:
  0.0 139.2 jit_solution(1958782363245564927)
XLA Ops:
  0.0 2.0 %fusion.49 = (bf16[32,1,2048]{2,1,0:T(2,128)(2,1)S(1)}, bf16[32,1,2048]{2,1,0:T(2,128)(2,1)S(1)}) fusion(bf16[32,64,2048]{2,1,0:T(8,128)(2,1)} %dens.1), kind=kLoop, calls=%fused_computation.66 | loop fusion | bytes 524288 | tf_op jit(solution)/shard_map/slice | solution.py:196
  2.0 0.1 copy.49
  2.1 1.3 collective-permute-start.2
  3.4 0.1 copy.48
  3.5 0.0 copy-start
  3.5 0.0 copy-start.1
  3.5 0.0 copy-start.2
  3.5 3.2 %collective-permute-start.3 = (bf16[32,2048]{1,0:T(8,128)(2,1)S(1)}, bf16[32,2048]{1,0:T(8,128)(2,1)S(1)}, u32[]{:S(2)}, u32[]{:S(2)}) collective-permute-start(bf16[32,2048]{1,0:T(8,128)(2,1)S(1)} %bitcast.79), channel_id=1, source_target_pairs={{0,1},{1,2},{2,3},{3,4},{4,5},{5,6},{6,7},{8,9},{9,10},{10,11},{11... | collective-permute-start | bytes 393224 | tf_op jit(solution)/shard_map/ppermute | solution.py:191
  6.7 1.1 slice_bitcast_fusion
  7.8 4.9 %collective-permute-start = (bf16[64,2048]{1,0:T(8,128)(2,1)S(1)}, bf16[64,2048]{1,0:T(8,128)(2,1)S(1)}, u32[]{:S(2)}, u32[]{:S(2)}) collective-permute-start(bf16[64,2048]{1,0:T(8,128)(2,1)S(1)} %get-tuple-element.11), channel_id=1, source_target_pairs={{0,8},{8,16},{16,24},{1,9},{9,17},{17,25},{2,10},{10,18},{18,26},{... | collective-permute-start | bytes 786440 | tf_op jit(solution)/shard_map/ppermute | solution.py:191
  12.6 1.3 collective-permute-start.1
  14.0 0.1 pad.2.clone
  14.0 0.0 collective-permute-done.2
  14.0 0.2 copy.36
  14.2 0.0 collective-permute-done.3
  14.3 0.2 copy.37
  14.5 0.9 maximum_maximum_fusion.yh
  15.4 3.7 %collective-permute-done.zlo = bf16[64,2048]{1,0:T(8,128)(2,1)S(1)} collective-permute-done((bf16[64,2048]{1,0:T(8,128)(2,1)S(1)}, bf16[64,2048]{1,0:T(8,128)(2,1)S(1)}, u32[]{:S(2)}, u32[]{:S(2)}) %collective-permute-start) | collective-permute-done | bytes 262176 | tf_op jit(solution)/shard_map/ppermute | solution.py:191
  19.1 7.6 %collective-permute-done.1.zhi = bf16[64,2048]{1,0:T(8,128)(2,1)S(1)} collective-permute-done((bf16[64,2048]{1,0:T(8,128)(2,1)S(1)}, bf16[64,2048]{1,0:T(8,128)(2,1)S(1)}, u32[]{:S(2)}, u32[]{:S(2)}) %collective-permute-start.1) | collective-permute-done | bytes 262176 | tf_op jit(solution)/shard_map/ppermute | solution.py:191
  26.6 0.0 copy-done
  26.7 0.0 copy-done.1
  26.7 0.0 copy-done.2
  26.7 43.8 %shard_map.64 = f32[4,64,2048]{2,1,0:T(8,128)S(1)} custom-call(s32[4]{0:T(128)S(1)} %copy-done.2, bf16[32,64,2048]{2,1,0:T(8,128)(2,1)} %dens.1, bf16[64,2048]{1,0:T(8,128)(2,1)S(1)} %collective-permute-done.zlo, bf16[64,2048]{1,0:T(8,128)(2,1)S(1)} %collective-permute-done.1.zhi, bf16[32,16,2048]{2,1,0:T(8,128)(2,1)S(1)} %maximum_maximum_fusion.yh, ...), custom_call_target="tpu_custom_call" | custom-call | tf_op jit(solution)/shard_map/pallas_call | solution.py:171
  70.5 1.6 %copy.38 = f32[4,4,16,2048]{3,2,0,1:T(8,128)} copy(f32[4,4,16,2048]{3,2,1,0:T(8,128)S(1)} %bitcast.75) | data formatting | bytes 4194304 | tf_op jit(solution)/shard_map/reshape | solution.py:209
  72.1 0.0 copy-start.6
  72.1 3.7 %all-to-all-start = ((f32[4,4,16,2048]{3,2,0,1:T(8,128)}), f32[4,4,16,2048]{3,2,0,1:T(8,128)S(1)}, u32[]{:S(2)}, u32[]{:S(2)}) async-start(f32[4,4,16,2048]{3,2,0,1:T(8,128)} %copy.38), calls=%async_computation | async-start | bytes 4194304 | tf_op jit(solution)/shard_map/all_to_all | solution.py:210
  75.8 0.0 copy-done.6
  75.8 0.2 convert_reduce_fusion.1
  76.0 0.1 fusion
  76.2 0.7 all_to_all.14
  76.9 24.3 %all-to-all-done = f32[4,4,16,2048]{3,2,0,1:T(8,128)S(1)} async-done(((f32[4,4,16,2048]{3,2,0,1:T(8,128)}), f32[4,4,16,2048]{3,2,0,1:T(8,128)S(1)}, u32[]{:S(2)}, u32[]{:S(2)}) %all-to-all-start) | async-done | bytes 2097184 | tf_op jit(solution)/shard_map/all_to_all | solution.py:210
  101.2 3.9 %all-to-all-start.2 = ((f32[8,1,2]{2,1,0:T(1,128)}), f32[8,1,2]{2,1,0:T(1,128)S(1)}, u32[]{:S(2)}, u32[]{:S(2)}) async-start(f32[8,1,2]{2,1,0:T(1,128)} %bitcast.13), calls=%async_computation.2 | async-start | bytes 8192 | tf_op jit(solution)/shard_map/all_to_all | solution.py:245
  105.2 0.7 mul.130
  105.9 0.7 mul.136
  106.6 0.9 fusion.51
  107.5 0.0 copy-start.3
  107.5 0.0 copy-start.4
  107.5 0.0 copy-start.5
  107.5 1.2 squeeze.33
  108.7 0.1 squeeze.34
  108.8 0.1 squeeze.35
  108.9 0.1 squeeze.36
  109.1 0.0 copy-done.3
  109.1 0.0 copy-done.4
  109.1 0.0 copy-done.5
  109.1 0.7 fusion.1
  109.9 1.5 %copy.39 = f32[8,2,3,4096]{3,1,2,0:T(2,128)} copy(f32[8,2,3,4096]{3,0,2,1:T(8,128)S(1)} %fusion.1) | data formatting | bytes 1572864 | tf_op jit(solution)/shard_map/sp,cpr->scr/dot_general | solution.py:237
  111.4 0.0 all-to-all-done.2
  111.4 5.1 %all-to-all-start.1 = ((f32[8,2,3,4096]{3,1,2,0:T(2,128)}), f32[8,2,3,4096]{3,1,2,0:T(2,128)S(1)}, u32[]{:S(2)}, u32[]{:S(2)}) async-start(f32[8,2,3,4096]{3,1,2,0:T(2,128)} %copy.39), calls=%async_computation.1 | async-start | bytes 1572864 | tf_op jit(solution)/shard_map/all_to_all | solution.py:244
  116.5 0.1 convert_element_type.21
  116.6 20.8 %all-to-all-done.1 = f32[8,2,3,4096]{3,1,2,0:T(2,128)S(1)} async-done(((f32[8,2,3,4096]{3,1,2,0:T(2,128)}), f32[8,2,3,4096]{3,1,2,0:T(2,128)S(1)}, u32[]{:S(2)}, u32[]{:S(2)}) %all-to-all-start.1) | async-done | bytes 786464 | tf_op jit(solution)/shard_map/all_to_all | solution.py:244
  137.4 0.1 copy.40
  137.5 0.5 reshape.133
  138.1 1.1 convolution_bitcast_fusion
  (9 shorter events, 0.2 us)
Async XLA Ops:
  2.1 12.0 %collective-permute-start.2 = (bf16[32,2048]{1,0:T(8,128)(2,1)S(1)}, bf16[32,2048]{1,0:T(8,128)(2,1)S(1)}, u32[]{:S(2)}, u32[]{:S(2)}) collective-permute-start(bf16[32,2048]{1,0:T(8,128)(2,1)S(1)} %bitcast.77), channel_id=1, source_target_pairs={{1,0},{2,1},{3,2},{4,3},{5,4},{6,5},{7,6},{9,8},{10,9},{11,10},{12... | collective-permute-start | bytes 393224 | tf_op jit(solution)/shard_map/ppermute | solution.py:191
  3.5 23.2 %copy-start = (bf16[512,256]{1,0:T(8,128)(2,1)S(1)}, bf16[512,256]{1,0:T(8,128)(2,1)}, u32[]{:S(2)}) copy-start(bf16[512,256]{1,0:T(8,128)(2,1)} %constant.47.clone.right) | copy-start | bytes 786436
  3.5 23.2 %copy-start.1 = (bf16[64,240]{1,0:T(8,128)(2,1)S(1)}, bf16[64,240]{1,0:T(8,128)(2,1)}, u32[]{:S(2)}) copy-start(bf16[64,240]{1,0:T(8,128)(2,1)} %constant.46.clone.left) | copy-start | bytes 92164
  3.5 23.2 %copy-start.2 = (s32[4]{0:T(128)S(1)}, s32[4]{0:T(128)}, u32[]{:S(2)}) copy-start(s32[4]{0:T(128)} %rank.1) | copy-start | bytes 52
  3.5 10.8 %collective-permute-start.3 = (bf16[32,2048]{1,0:T(8,128)(2,1)S(1)}, bf16[32,2048]{1,0:T(8,128)(2,1)S(1)}, u32[]{:S(2)}, u32[]{:S(2)}) collective-permute-start(bf16[32,2048]{1,0:T(8,128)(2,1)S(1)} %bitcast.79), channel_id=1, source_target_pairs={{0,1},{1,2},{2,3},{3,4},{4,5},{5,6},{6,7},{8,9},{9,10},{10,11},{11... | collective-permute-start | bytes 393224 | tf_op jit(solution)/shard_map/ppermute | solution.py:191
  7.8 11.3 %collective-permute-start = (bf16[64,2048]{1,0:T(8,128)(2,1)S(1)}, bf16[64,2048]{1,0:T(8,128)(2,1)S(1)}, u32[]{:S(2)}, u32[]{:S(2)}) collective-permute-start(bf16[64,2048]{1,0:T(8,128)(2,1)S(1)} %get-tuple-element.11), channel_id=1, source_target_pairs={{0,8},{8,16},{16,24},{1,9},{9,17},{17,25},{2,10},{10,18},{18,26},{... | collective-permute-start | bytes 786440 | tf_op jit(solution)/shard_map/ppermute | solution.py:191
  12.6 14.0 %collective-permute-start.1 = (bf16[64,2048]{1,0:T(8,128)(2,1)S(1)}, bf16[64,2048]{1,0:T(8,128)(2,1)S(1)}, u32[]{:S(2)}, u32[]{:S(2)}) collective-permute-start(bf16[64,2048]{1,0:T(8,128)(2,1)S(1)} %get-tuple-element.10), channel_id=1, source_target_pairs={{8,0},{16,8},{24,16},{9,1},{17,9},{25,17},{10,2},{18,10},{26,18},{... | collective-permute-start | bytes 786440 | tf_op jit(solution)/shard_map/ppermute | solution.py:191
  72.1 3.8 %copy-start.6 = (s32[8]{0:T(128)S(1)}, s32[8]{0:T(128)}, u32[]{:S(2)}) copy-start(s32[8]{0:T(128)} %param.8) | copy-start | bytes 100
  72.1 29.1 %all-to-all-start = ((f32[4,4,16,2048]{3,2,0,1:T(8,128)}), f32[4,4,16,2048]{3,2,0,1:T(8,128)S(1)}, u32[]{:S(2)}, u32[]{:S(2)}) async-start(f32[4,4,16,2048]{3,2,0,1:T(8,128)} %copy.38), calls=%async_computation | async-start | bytes 4194304 | tf_op jit(solution)/shard_map/all_to_all | solution.py:210
  101.2 10.2 %all-to-all-start.2 = ((f32[8,1,2]{2,1,0:T(1,128)}), f32[8,1,2]{2,1,0:T(1,128)S(1)}, u32[]{:S(2)}, u32[]{:S(2)}) async-start(f32[8,1,2]{2,1,0:T(1,128)} %bitcast.13), calls=%async_computation.2 | async-start | bytes 8192 | tf_op jit(solution)/shard_map/all_to_all | solution.py:245
  107.5 1.6 %copy-start.3 = (f32[8,4096]{1,0:T(8,128)S(1)}, f32[8,4096]{1,0:T(8,128)}, u32[]{:S(2)}) copy-start(f32[8,4096]{1,0:T(8,128)} %mul.130) | copy-start | bytes 393220
  107.5 1.6 %copy-start.4 = (f32[8,4096]{1,0:T(8,128)S(1)}, f32[8,4096]{1,0:T(8,128)}, u32[]{:S(2)}) copy-start(f32[8,4096]{1,0:T(8,128)} %mul.136) | copy-start | bytes 393220
  107.5 1.6 %copy-start.5 = (f32[3]{0:T(128)S(1)}, f32[3]{0:T(128)}, u32[]{:S(2)}) copy-start(f32[3]{0:T(128)} %constant.48.clone) | copy-start | bytes 40
  111.4 26.0 %all-to-all-start.1 = ((f32[8,2,3,4096]{3,1,2,0:T(2,128)}), f32[8,2,3,4096]{3,1,2,0:T(2,128)S(1)}, u32[]{:S(2)}, u32[]{:S(2)}) async-start(f32[8,2,3,4096]{3,1,2,0:T(2,128)} %copy.39), calls=%async_computation.1 | async-start | bytes 1572864 | tf_op jit(solution)/shard_map/all_to_all | solution.py:244

commit v2 on v1

v2 whole, which is shorter than its diff:
```python
import math
import jax
import jax.numpy as jnp
import numpy as np
from jax import lax
from jax.experimental import pallas as pl
from jax.experimental.pallas import tpu as pltpu
from jax.sharding import PartitionSpec as P

MOST = 2

EXTINCT = 0.5
LIGHT_Z = 0.6
LIGHT_Y = 0.48
LIGHT_X = 0.64
SHARPNESS = 6.0
BACKDROP = (0.08, 0.1, 0.14)

PAD = 128
CB = 256
RB = 16
SIG_A = math.exp(-3.0)
SIG_B = math.exp(-2.5)
COS = (1.9999999935320312, -0.9999997751464547, 0.08333208188264607,
       -0.002775337047259153, 4.7654375196060637e-05)


def stencils(rows):
    wy, wz = LIGHT_Y / LIGHT_X, LIGHT_Z / LIGHT_X
    left = np.zeros((rows, 3 * rows), np.float32)
    for r in range(rows):
        left[r, r] = -wz
        left[r, 2 * rows + r] = wz
        if r < rows - 1:
            left[r, rows + r + 1] = wy
        if r > 0:
            left[r, rows + r - 1] = -wy
    right = np.zeros((CB + 2 * PAD, CB), np.float32)
    for c in range(CB):
        right[c + PAD + 1, c] = 1.0
        right[c + PAD - 1, c] = -1.0
    return jnp.asarray(left, jnp.bfloat16), jnp.asarray(right, jnp.bfloat16)


def make_facing(d, g, dens32, hs, left, right, cells, rows, zc):
    wy = LIGHT_Y / LIGHT_X

    def facing(block, slot, chunk):
        z0 = chunk * zc
        c0 = pl.multiple_of(block * CB, CB)
        wide = d[pl.ds(z0 + 1, zc), :, pl.ds(c0, CB + 2 * PAD)]
        dx = jnp.dot(wide.reshape(zc * rows, CB + 2 * PAD), right[...],
                     preferred_element_type=jnp.float32)
        c1 = pl.multiple_of(block * CB + PAD, PAD)
        sub = lax.broadcasted_iota(jnp.int32, (8, CB), 0)
        for i in range(zc):
            tall = d[pl.ds(z0 + i, 3), :, pl.ds(c1, CB)].reshape(3 * rows, CB)
            dyz = jnp.dot(left[...], tall, preferred_element_type=jnp.float32)
            both = dyz + dx[i * rows:(i + 1) * rows]
            low = hs[0, pl.ds(z0 + i, 1), :] * wy
            high = hs[1, pl.ds(z0 + i, 1), :] * wy
            g[slot, z0 + i, 0:8] = both[0:8] - jnp.where(sub == 0, low, 0.0)
            g[slot, z0 + i, 8:rows - 8] = both[8:rows - 8]
            g[slot, z0 + i, rows - 8:rows] = both[rows - 8:] + jnp.where(sub == 7, high, 0.0)
            dens32[slot, z0 + i] = wide[i, :, PAD:PAD + CB].astype(jnp.float32)

    return facing


def march(dens32, g, state, ascend, slot, rb, half, halves, cells):
    steps = cells // halves
    first = half == 0
    trans = jnp.where(first, 1.0, state[0])
    total, m0, m1, wave = (jnp.where(first, 0.0, state[i]) for i in range(1, 5))
    r0 = pl.multiple_of(rb * RB, RB)
    bias = (0.35 + 0.65 * 0.5) / (0.65 * 0.5)
    for i in range(steps):
        k = half * steps + i
        z = jnp.where(ascend, k, cells - 1 - k)
        dens = dens32[slot, z, pl.ds(r0, RB), :]
        face = g[slot, z, pl.ds(r0, RB), :]
        shade = jnp.tanh(face * (0.5 * SHARPNESS * LIGHT_X)) + bias
        after = trans * jnp.exp2(dens * (-EXTINCT * math.log2(math.e)))
        ws = (trans - after) * shade
        trans = after
        u = dens + 0.01
        wr = ws / ((u + SIG_A) * (u + SIG_B))
        x = jnp.log(u) * (1.7 / 4) + math.pi / 4
        s = x * x
        c = COS[4] * s + COS[3]
        c = c * s + COS[2]
        c = c * s + COS[1]
        c = c * s + COS[0]
        v = c * c - 2.0
        total = total + ws
        m0 = m0 + wr
        m1 = m1 + wr * u
        wave = wave + ws * (v * v)
    for i, val in enumerate((trans, total, m0, m1, wave)):
        state[i] = val
    scale = 0.65 * 0.5
    return (
        scale * (total - SIG_A * (m1 + SIG_B * m0)),
        scale * (total - 0.25 * wave),
        scale * SIG_B * (m1 + SIG_A * m0),
        trans,
    )


def brick_kernel(nd, nt, rank, route, dens, ysend, labels, left, right, inbox, arrived,
                 d, hb, hs, g, dens32, state, out, recv, fin, outbox,
                 dens_sem, hsend, hrecv, dsend, drecv, tsend, trecv, lsend, lrecv):
    cells, rows, cols = dens.shape
    nb, bands, halves = cols // CB, rows // RB, 2
    its = bands * halves
    zc = cells // its
    qrows = rows // nd
    width, rpp = outbox.shape[3], outbox.shape[2] // MOST
    groups = tsend.shape[0]
    me_d, me_t = lax.axis_index("depth"), lax.axis_index("tile")
    mesh_ids = pl.DeviceIdType.MESH

    barrier = pltpu.get_barrier_semaphore()

    @pl.loop(1, nt)
    def _(o):
        pl.semaphore_signal(barrier, inc=1, device_id=(me_d, lax.rem(me_t + o, nt)), device_id_type=mesh_ids)

    for k in range(1, nd):
        pl.semaphore_signal(barrier, inc=1, device_id=(lax.rem(me_d + k, nd), me_t), device_id_type=mesh_ids)

    def cols_of(b):
        return pl.ds(pl.multiple_of(b * CB, CB), CB)

    def pads_of(b):
        return pl.ds(pl.multiple_of(b * CB + PAD, PAD), CB)

    def dens_copy(b):
        return pltpu.make_async_copy(
            dens.at[:, :, cols_of(b)], d.at[pl.ds(1, cells), :, pads_of(b)], dens_sem.at[b])

    def halo(kind, b):
        src, dst, step = (
            (dens.at[cells - 1, :, cols_of(b)], d.at[0, :, pads_of(b)], 1),
            (dens.at[0, :, cols_of(b)], d.at[cells + 1, :, pads_of(b)], nd - 1),
            (ysend.at[0, :, cols_of(b)], hb.at[0, :, cols_of(b)], 1),
            (ysend.at[1, :, cols_of(b)], hb.at[1, :, cols_of(b)], nt - 1),
        )[kind]
        to = (lax.rem(me_d + step, nd), me_t) if kind < 2 else (me_d, lax.rem(me_t + step, nt))
        return pltpu.make_async_remote_copy(
            src_ref=src, dst_ref=dst, send_sem=hsend.at[kind, b], recv_sem=hrecv.at[kind, b],
            device_id=to, device_id_type=mesh_ids)

    sends = (me_d < nd - 1, me_d > 0, me_t < nt - 1, me_t > 0)
    gets = (me_d > 0, me_d < nd - 1, me_t > 0, me_t < nt - 1)

    @pl.loop(0, nb)
    def _(b):
        dens_copy(b).start()

    side = jnp.zeros((cells + 2, rows, PAD), d.dtype)
    d[:, :, :PAD] = side
    d[:, :, cols + PAD:] = side

    @pl.when(me_d == 0)
    def _():
        d[0, :, PAD:cols + PAD] = jnp.zeros((rows, cols), d.dtype)

    @pl.when(me_d == nd - 1)
    def _():
        d[cells + 1, :, PAD:cols + PAD] = jnp.zeros((rows, cols), d.dtype)

    @pl.when(me_t == 0)
    def _():
        hb[0] = jnp.zeros((cells, cols), hb.dtype)

    @pl.when(me_t == nt - 1)
    def _():
        hb[1] = jnp.zeros((cells, cols), hb.dtype)

    pl.semaphore_wait(barrier, nt - 1 + nd - 1)

    for kind in range(4):
        @pl.when(sends[kind])
        def _():
            @pl.loop(0, nb)
            def _(b):
                halo(kind, b).start()

    def label_copy(o):
        return pltpu.make_async_remote_copy(
            src_ref=labels.at[o], dst_ref=arrived.at[o], send_sem=lsend.at[o], recv_sem=lrecv.at[o],
            device_id=(me_d, lax.rem(me_t + o, nt)), device_id_type=mesh_ids)

    own_labels = pltpu.make_async_copy(labels.at[0], arrived.at[0], lsend.at[0])
    own_labels.start()

    @pl.loop(1, nt)
    def _(o):
        label_copy(o).start()

    def arrive(b):
        dens_copy(b).wait()
        for kind in range(4):
            @pl.when(gets[kind])
            def _():
                halo(kind, b).wait_recv()

    def spread(b):
        hs[...] = hb[:, :, cols_of(b)].astype(jnp.float32)

    ascend = rank[0] == 0
    facing = make_facing(d, g, dens32, hs, left, right, cells, rows, zc)

    def depth_copy(k, b, src):
        to = lax.rem(me_d + k, nd)
        return pltpu.make_async_remote_copy(
            src_ref=out.at[:, pl.ds(pl.multiple_of(to * qrows, 8), qrows), cols_of(b)],
            dst_ref=recv.at[src, :, :, cols_of(b)],
            send_sem=dsend.at[b, k], recv_sem=drecv.at[b, src],
            device_id=(to, me_t), device_id_type=mesh_ids)

    def depth_send(b):
        for k in range(1, nd):
            depth_copy(k, b, me_d).start()
        mine = out[:, pl.ds(pl.multiple_of(me_d * qrows, 8), qrows), cols_of(b)]
        recv[me_d, :, :, cols_of(b)] = mine

    def composite(b):
        for k in range(1, nd):
            depth_copy(k, b, lax.rem(me_d + k, nd)).wait_recv()
        color = recv[0, 0:3, :, cols_of(b)]
        trans = recv[0, 3, :, cols_of(b)]
        for i in range(1, nd):
            new = recv[i, 0:3, :, cols_of(b)]
            new_trans = recv[i, 3, :, cols_of(b)]
            front, back = jnp.where(ascend, color, new), jnp.where(ascend, new, color)
            color = front + jnp.where(ascend, trans, new_trans)[None] * back
            trans = trans * new_trans
        for ch in range(3):
            fin[ch, :, cols_of(b)] = color[ch] + trans * BACKDROP[ch]

    def tile_copy(o, part, window):
        return pltpu.make_async_remote_copy(
            src_ref=outbox.at[o, :, :, window], dst_ref=inbox.at[o, :, :, window],
            send_sem=tsend.at[part, o], recv_sem=trecv.at[part, o],
            device_id=(me_d, lax.rem(me_t + o, nt)), device_id_type=mesh_ids)

    def tile_own(part, window):
        return pltpu.make_async_copy(
            outbox.at[0, :, :, window], inbox.at[0, :, :, window], tsend.at[part, 0])

    def ship(part, window):
        @pl.loop(0, nt)
        def _(o):
            for m in range(MOST):
                p = route[o * MOST + m]
                for r in range(rpp):
                    if width == cols:
                        piece = fin[:, pl.ds(p * rpp + r, 1), window]
                    else:
                        per = cols // width
                        c = pl.multiple_of(lax.rem(p, per) * width, width)
                        piece = fin[:, pl.ds(lax.div(p, per), 1), pl.ds(c, width)]
                    outbox[o, :, m * rpp + r:m * rpp + r + 1, window] = piece

        tile_own(part, window).start()

        @pl.loop(1, nt)
        def _(o):
            tile_copy(o, part, window).start()

    arrive(0)
    arrive(1)
    spread(0)

    @pl.loop(0, its)
    def _(it):
        facing(0, 0, it)

    def finish(b):
        composite(b)
        if groups == nb:
            ship(b, cols_of(b))

    @pl.loop(0, nb)
    def _(b):
        @pl.when(b + 2 < nb)
        def _():
            arrive(b + 2)

        slot = lax.rem(b, 2)
        ahead = lax.rem(b + 1, nb)
        spread(ahead)

        @pl.loop(0, its)
        def _(it):
            facing(ahead, 1 - slot, it)
            rb = lax.div(it, halves)
            vals = march(dens32, g, state, ascend, slot, rb, lax.rem(it, halves), halves, cells)
            for ch, val in enumerate(vals):
                out[ch, pl.ds(pl.multiple_of(rb * RB, RB), RB), cols_of(b)] = val

        depth_send(b)

        @pl.when(b > 0)
        def _():
            finish(b - 1)

    finish(nb - 1)
    if groups != nb:
        ship(0, pl.ds(0, width))

    own_labels.wait()

    @pl.loop(1, nt)
    def _(o):
        label_copy(o).wait()

    @pl.loop(0, groups)
    def _(part):
        window = cols_of(part) if groups == nb else pl.ds(0, width)
        tile_own(part, window).wait()

        @pl.loop(1, nt)
        def _(o):
            tile_copy(o, part, window).wait()

    @pl.loop(0, nb)
    def _(b):
        for k in range(1, nd):
            depth_copy(k, b, me_d).wait_send()

    for kind in range(4):
        @pl.when(sends[kind])
        def _():
            @pl.loop(0, nb)
            def _(b):
                halo(kind, b).wait_send()


def place_kernel(arrived, inbox, display):
    nt, rpp, width = inbox.shape[0], inbox.shape[2] // MOST, inbox.shape[3]

    @pl.loop(0, nt)
    def _(o):
        for m in range(MOST):
            label = arrived[o, 0, m]

            @pl.when(label >= 0)
            def _():
                for r in range(rpp):
                    piece = inbox[o, :, m * rpp + r:m * rpp + r + 1, :]
                    display[:, 0, pl.ds(label, 1), r * width:(r + 1) * width] = piece


def on_device(density, depth_rank, piece_home):
    cells, rows, cols = density.shape
    nd, nt = lax.axis_size("depth"), lax.axis_size("tile")
    ppd = piece_home.shape[0]
    qrows = rows // nd
    piece_len = qrows * cols // ppd
    width = min(piece_len, cols)
    rpp = piece_len // width
    nb = cols // CB
    groups = nb if width == cols else 1

    order = jnp.arange(ppd, dtype=jnp.int32)
    owners = piece_home // ppd
    shared = (owners[:, None] == owners[None, :]) & (order[None, :] < order[:, None])
    earlier = jnp.sum(shared.astype(jnp.int32), axis=1)
    target = ((owners - lax.axis_index("tile") + nt) % nt) * MOST + earlier
    hit = jnp.arange(nt * MOST, dtype=jnp.int32)[:, None] == target[None, :]
    route = jnp.sum(jnp.where(hit, order[None, :], 0), axis=1)
    label = jnp.sum(jnp.where(hit, piece_home[None, :] % ppd + 1, 0), axis=1) - 1
    labels = jnp.pad(label.reshape(nt, 1, MOST), ((0, 0), (0, 0), (0, 128 - MOST)))

    ysend = jnp.stack([density[:, rows - 1], density[:, 0]])
    left, right = stencils(rows)
    anyspec = pl.BlockSpec(memory_space=pl.ANY)
    vmem = pl.BlockSpec(memory_space=pltpu.VMEM)
    smem = pl.BlockSpec(memory_space=pltpu.SMEM)
    dma = pltpu.SemaphoreType.DMA
    f32 = jnp.float32
    inbox, arrived = pl.pallas_call(
        lambda *refs: brick_kernel(nd, nt, *refs),
        out_shape=(jax.ShapeDtypeStruct((nt, 3, MOST * rpp, width), f32),
                   jax.ShapeDtypeStruct((nt, 1, 128), jnp.int32)),
        in_specs=[smem, smem, anyspec, anyspec, anyspec, vmem, vmem],
        out_specs=(anyspec, anyspec),
        scratch_shapes=[
            pltpu.VMEM((cells + 2, rows, cols + 2 * PAD), jnp.bfloat16),
            pltpu.VMEM((2, cells, cols), jnp.bfloat16),
            pltpu.VMEM((2, cells, CB), f32),
            pltpu.VMEM((2, cells, rows, CB), f32),
            pltpu.VMEM((2, cells, rows, CB), f32),
            pltpu.VMEM((5, RB, CB), f32),
            pltpu.VMEM((4, rows, cols), f32),
            pltpu.VMEM((nd, 4, qrows, cols), f32),
            pltpu.VMEM((3, qrows, cols), f32),
            pltpu.VMEM((nt, 3, MOST * rpp, width), f32),
            dma((nb,)), dma((4, nb)), dma((4, nb)), dma((nb, nd)), dma((nb, nd)),
            dma((groups, nt)), dma((groups, nt)), dma((nt,)), dma((nt,)),
        ],
        compiler_params=pltpu.CompilerParams(
            collective_id=0, has_side_effects=True, vmem_limit_bytes=56 * 1024 * 1024),
    )(depth_rank, route, density, ysend, labels, left, right)
    return pl.pallas_call(
        place_kernel,
        out_shape=jax.ShapeDtypeStruct((3, 1, ppd, piece_len), f32),
        in_specs=[smem, vmem],
        out_specs=vmem,
    )(arrived, inbox)


def solution(mesh):
    in_specs = (P("depth", "tile", None), P(), P("tile"))
    out_specs = P(None, "depth", "tile", None)
    return jax.shard_map(
        on_device, mesh=mesh, in_specs=in_specs, out_specs=out_specs, check_vma=False
    )
```

time: 140 us -> 73.4 us (0.52)
  waiting for transfers between devices: 56.4 us -> 0 us
  Pallas kernels: 43.8 us -> 68.2 us
  starting transfers between devices: 23.3 us -> 0 us
  local copies, waits for them, and re-layouts: 12.1 us -> 2.8 us
  matrix products: 1.98 us -> 0 us
    all_to_all x3 -> x0, waiting for transfers between devices: 45.2 us -> none  [the longest x1 24.3 us: on_device(): lax.all_to_all(layered, 'depth', split_axis=1, concat_axis=1, tiled=True)]
    pallas_call x1 -> x2, Pallas kernels: 43.8 us -> 68.2 us  [the longest x1 66 us: on_device(): pl.pallas_call(lambda *refs: brick_kernel(nd, nt, *refs), out_shape=(jax....]
    all_to_all x3 -> x0, starting transfers between devices: 12.7 us -> none  [the longest x1 5.1 us: on_device(): lax.all_to_all(outbox, 'tile', split_axis=0, concat_axis=0, tiled=True)]
    ppermute x4 -> x0, waiting for transfers between devices: 11.3 us -> none  [move(): lax.ppermute(x, axis, [(i, i + step) for i in range(n) if 0 <= i + step <...]
    ppermute x4 -> x0, starting transfers between devices: 10.6 us -> none  [move(): lax.ppermute(x, axis, [(i, i + step) for i in range(n) if 0 <= i + step <...]
    squeeze x5 -> x0, local copies, waits for them, and re-layouts: 2.62 us -> none  [the longest x1 1.17 us: on_device(): color_acc = gathered[:3, 0]]
    reshape x2 -> x0, local copies, waits for them, and re-layouts: 2.1 us -> none  [the longest x1 1.56 us: on_device(): partial_image.reshape(4, depth_count, row_count // depth_count, columns)]
    dot_general x3 -> x0, matrix products: 1.98 us -> none  [the longest x1 1.12 us: on_device(): jnp.einsum('qs,scr->cqr', placing, flat_pieces, precision=lax.Precision.H...]
  transfers between devices with their start and end apart: 7 -> 0, of which waited for: 4 -> 0; matrix products, arithmetic and copies ran while one was open for 7% -> 0% of each run, Pallas kernels for 0% -> 0%
where the time goes in v2:
time: 73.4 us; the launch traced here: 73.2 us
  Pallas kernels  68.2 us (93%)
  local copies, waits for them, and re-layouts  2.8 us (4%)
  other arithmetic  2.21 us (3%)
    pallas_call x1, Pallas kernels, on_device(): pl.pallas_call(lambda *refs: brick_kernel(nd, nt, *refs), out_shape=(jax....  66 us
    pallas_call x1, Pallas kernels, on_device(): pl.pallas_call(place_kernel, out_shape=jax.ShapeDtypeStruct((3, 1, ppd, p...  2.13 us
    slice x1, local copies, waits for them, and re-layouts, on_device(): ysend = jnp.stack([density[:, rows - 1], density[:, 0]])  1.97 us

profile of v2, /device:TPU:0, one launch (start us, length us, event | category | flops | bytes accessed | tf_op | source)
XLA Modules:
  0.0 73.2 jit_solution(3165366016320042561)
XLA Ops:
  0.0 0.7 and_select_fusion.2
  0.7 0.2 convert_reduce_fusion
  0.9 0.6 select_reduce_fusion
  1.5 0.1 sub.19
  1.6 0.6 pad.4.refs_4_
  2.2 2.0 %fusion.5 = (bf16[32,1,2048]{2,1,0:T(2,128)(2,1)S(1)}, bf16[32,1,2048]{2,1,0:T(2,128)(2,1)S(1)}) fusion(bf16[32,64,2048]{2,1,0:T(8,128)(2,1)} %refs_2_.1), kind=kLoop, calls=%fused_computation.22 | loop fusion | bytes 524288 | tf_op jit(solution)/shard_map/slice | solution.py:378
  4.1 0.2 copy_bitcast_fusion
  4.3 0.7 pad_maximum_fusion.refs_3_
  5.0 66.0 %shard_map.55 = (f32[8,3,4,2048]{3,2,1,0:T(4,128)}, s32[8,1,128]{2,1,0:T(1,128)}) custom-call(s32[4]{0:T(128)} %refs_0_.1, s32[16]{0:T(128)} %get-tuple-element.10.refs_1_, bf16[32,64,2048]{2,1,0:T(8,128)(2,1)} %refs_2_.1, bf16[2,32,2048]{2,1,0:T(8,128)(2,1)} %pad_maximum_fusion.refs_3_, s32[8,1,128]{2,1,0:T(1,128)} %pad.4.refs_4_, ...), custom_call_target="tpu_custom_call" | custom-call | tf_op jit(solution)/shard_map/pallas_call | solution.py:385
  71.1 2.1 %shard_map.56 = f32[3,1,8,4096]{3,2,1,0:T(8,128)} custom-call(s32[8,1,128]{2,1,0:T(1,128)} %get-tuple-element.7.arrived, f32[8,3,4,2048]{3,2,1,0:T(4,128)} %get-tuple-element.8.inbox), custom_call_target="tpu_custom_call" | custom-call | tf_op jit(solution)/shard_map/pallas_call | solution.py:408
  (2 shorter events, 0.0 us)

commit v3 on v2

--- a/solution.py
+++ b/solution.py
@@ -8,6 +8,7 @@
 from jax.sharding import PartitionSpec as P
 
 MOST = 2
+EMPTY = -(2**30)
 
 EXTINCT = 0.5
 LIGHT_Z = 0.6
@@ -18,11 +19,19 @@
 
 PAD = 128
 CB = 256
-RB = 16
+MC = 128
 SIG_A = math.exp(-3.0)
 SIG_B = math.exp(-2.5)
-COS = (1.9999999935320312, -0.9999997751464547, 0.08333208188264607,
-       -0.002775337047259153, 4.7654375196060637e-05)
+SIN = (0.9999999978529928,
+       -0.1666666388441264,
+       0.008333274854744043,
+       -0.00019836767087186654,
+       2.7400072109094996e-06,
+       -2.2499595606831132e-08)
+
+
+def inverse(x):
+    return 1.0 / x
 
 
 def stencils(rows):
@@ -42,11 +51,12 @@
     return jnp.asarray(left, jnp.bfloat16), jnp.asarray(right, jnp.bfloat16)
 
 
-def make_facing(d, g, dens32, hs, left, right, cells, rows, zc):
+def make_facing(d, g_pair, dens_pair, hs, left, right, cells, rows, zc):
     wy = LIGHT_Y / LIGHT_X
 
     def facing(block, slot, chunk):
         z0 = chunk * zc
+        g, dens32 = g_pair[slot], dens_pair[slot]
         c0 = pl.multiple_of(block * CB, CB)
         wide = d[pl.ds(z0 + 1, zc), :, pl.ds(c0, CB + 2 * PAD)]
         dx = jnp.dot(wide.reshape(zc * rows, CB + 2 * PAD), right[...],
@@ -59,60 +69,61 @@
             both = dyz + dx[i * rows:(i + 1) * rows]
             low = hs[0, pl.ds(z0 + i, 1), :] * wy
             high = hs[1, pl.ds(z0 + i, 1), :] * wy
-            g[slot, z0 + i, 0:8] = both[0:8] - jnp.where(sub == 0, low, 0.0)
-            g[slot, z0 + i, 8:rows - 8] = both[8:rows - 8]
-            g[slot, z0 + i, rows - 8:rows] = both[rows - 8:] + jnp.where(sub == 7, high, 0.0)
-            dens32[slot, z0 + i] = wide[i, :, PAD:PAD + CB].astype(jnp.float32)
+            g[z0 + i, 0:8] = both[0:8] - jnp.where(sub == 0, low, 0.0)
+            g[z0 + i, 8:rows - 8] = both[8:rows - 8]
+            g[z0 + i, rows - 8:rows] = both[rows - 8:] + jnp.where(sub == 7, high, 0.0)
+            dens32[z0 + i] = wide[i, :, PAD:PAD + CB].astype(jnp.float32)
 
     return facing
 
 
-def march(dens32, g, state, ascend, slot, rb, half, halves, cells):
+def march(dens32, g, state, ascend, band, half, halves, cells, c0):
     steps = cells // halves
     first = half == 0
-    trans = jnp.where(first, 1.0, state[0])
-    total, m0, m1, wave = (jnp.where(first, 0.0, state[i]) for i in range(1, 5))
-    r0 = pl.multiple_of(rb * RB, RB)
+    lanes = slice(c0, c0 + MC)
+    trans = jnp.where(first, 1.0, state[0, :, lanes])
+    total, m0, m1, wave = (jnp.where(first, 0.0, state[i, :, lanes]) for i in range(1, 5))
+    band_rows = state.shape[1]
+    r0 = pl.multiple_of(band * band_rows, 8)
     bias = (0.35 + 0.65 * 0.5) / (0.65 * 0.5)
     for i in range(steps):
         k = half * steps + i
         z = jnp.where(ascend, k, cells - 1 - k)
-        dens = dens32[slot, z, pl.ds(r0, RB), :]
-        face = g[slot, z, pl.ds(r0, RB), :]
+        dens = dens32[z, pl.ds(r0, band_rows), lanes]
+        face = g[z, pl.ds(r0, band_rows), lanes]
         shade = jnp.tanh(face * (0.5 * SHARPNESS * LIGHT_X)) + bias
         after = trans * jnp.exp2(dens * (-EXTINCT * math.log2(math.e)))
         ws = (trans - after) * shade
         trans = after
         u = dens + 0.01
-        wr = ws / ((u + SIG_A) * (u + SIG_B))
-        x = jnp.log(u) * (1.7 / 4) + math.pi / 4
-        s = x * x
-        c = COS[4] * s + COS[3]
-        c = c * s + COS[2]
-        c = c * s + COS[1]
-        c = c * s + COS[0]
-        v = c * c - 2.0
+        wr = ws * inverse((u + SIG_A) * (u + SIG_B))
+        y = jnp.log(u) * (1.7 / 2) + math.pi / 2
+        q = y * y
+        c = SIN[-1]
+        for coef in SIN[-2::-1]:
+            c = c * q + coef
+        c = c * y
         total = total + ws
         m0 = m0 + wr
         m1 = m1 + wr * u
-        wave = wave + ws * (v * v)
+        wave = wave + ws * (c * c)
     for i, val in enumerate((trans, total, m0, m1, wave)):
-        state[i] = val
+        state[i, :, lanes] = val
     scale = 0.65 * 0.5
     return (
         scale * (total - SIG_A * (m1 + SIG_B * m0)),
-        scale * (total - 0.25 * wave),
+        scale * wave,
         scale * SIG_B * (m1 + SIG_A * m0),
         trans,
     )
 
 
-def brick_kernel(nd, nt, rank, route, dens, ysend, labels, left, right, inbox, arrived,
-                 d, hb, hs, g, dens32, state, out, recv, fin, outbox,
+def brick_kernel(nd, nt, pieces, rank, route, dens, ylast, yfirst, labels, left, right, inbox, arrived,
+                 d, hb, hs, g0, g1, dens0, dens1, state, out, recv, fin, outbox,
                  dens_sem, hsend, hrecv, dsend, drecv, tsend, trecv, lsend, lrecv):
     cells, rows, cols = dens.shape
-    nb, bands, halves = cols // CB, rows // RB, 2
-    its = bands * halves
+    nb, halves = cols // CB, 2
+    its = nd * halves
     zc = cells // its
     qrows = rows // nd
     width, rpp = outbox.shape[3], outbox.shape[2] // MOST
@@ -143,8 +154,8 @@
         src, dst, step = (
             (dens.at[cells - 1, :, cols_of(b)], d.at[0, :, pads_of(b)], 1),
             (dens.at[0, :, cols_of(b)], d.at[cells + 1, :, pads_of(b)], nd - 1),
-            (ysend.at[0, :, cols_of(b)], hb.at[0, :, cols_of(b)], 1),
-            (ysend.at[1, :, cols_of(b)], hb.at[1, :, cols_of(b)], nt - 1),
+            (ylast.at[:, cols_of(b)], hb.at[0, :, cols_of(b)], 1),
+            (yfirst.at[:, cols_of(b)], hb.at[1, :, cols_of(b)], nt - 1),
         )[kind]
         to = (lax.rem(me_d + step, nd), me_t) if kind < 2 else (me_d, lax.rem(me_t + step, nt))
         return pltpu.make_async_remote_copy(
@@ -180,11 +191,11 @@
 
     pl.semaphore_wait(barrier, nt - 1 + nd - 1)
 
-    for kind in range(4):
-        @pl.when(sends[kind])
-        def _():
-            @pl.loop(0, nb)
-            def _(b):
+    @pl.loop(0, nb)
+    def _(b):
+        for kind in range(4):
+            @pl.when(sends[kind])
+            def _():
                 halo(kind, b).start()
 
     def label_copy(o):
@@ -210,7 +221,8 @@
         hs[...] = hb[:, :, cols_of(b)].astype(jnp.float32)
 
     ascend = rank[0] == 0
-    facing = make_facing(d, g, dens32, hs, left, right, cells, rows, zc)
+    g_pair, dens_pair = (g0, g1), (dens0, dens1)
+    facing = make_facing(d, g_pair, dens_pair, hs, left, right, cells, rows, zc)
 
     def depth_copy(k, b, src):
         to = lax.rem(me_d + k, nd)
@@ -220,9 +232,7 @@
             send_sem=dsend.at[b, k], recv_sem=drecv.at[b, src],
             device_id=(to, me_t), device_id_type=mesh_ids)
 
-    def depth_send(b):
-        for k in range(1, nd):
-            depth_copy(k, b, me_d).start()
+    def keep_own(b):
         mine = out[:, pl.ds(pl.multiple_of(me_d * qrows, 8), qrows), cols_of(b)]
         recv[me_d, :, :, cols_of(b)] = mine
 
@@ -254,7 +264,8 @@
         @pl.loop(0, nt)
         def _(o):
             for m in range(MOST):
-                p = route[o * MOST + m]
+                p = lax.div((2 * m - 1) * route[o, 0, m], pieces)
+                p = jnp.where(route[o, 0, m] == EMPTY, 0, p)
                 for r in range(rpp):
                     if width == cols:
                         piece = fin[:, pl.ds(p * rpp + r, 1), window]
@@ -283,29 +294,40 @@
         if groups == nb:
             ship(b, cols_of(b))
 
-    @pl.loop(0, nb)
-    def _(b):
+    def step(b, slot):
         @pl.when(b + 2 < nb)
         def _():
             arrive(b + 2)
 
-        slot = lax.rem(b, 2)
         ahead = lax.rem(b + 1, nb)
         spread(ahead)
 
         @pl.loop(0, its)
         def _(it):
             facing(ahead, 1 - slot, it)
-            rb = lax.div(it, halves)
-            vals = march(dens32, g, state, ascend, slot, rb, lax.rem(it, halves), halves, cells)
-            for ch, val in enumerate(vals):
-                out[ch, pl.ds(pl.multiple_of(rb * RB, RB), RB), cols_of(b)] = val
-
-        depth_send(b)
+            k = lax.div(it, halves) + 1
+            half = lax.rem(it, halves)
+            band = lax.rem(me_d + k, nd)
+            for c0 in range(0, CB, MC):
+                vals = march(dens_pair[slot], g_pair[slot], state, ascend, band, half, halves, cells, c0)
+                lanes = pl.ds(pl.multiple_of(b * CB + c0, MC), MC)
+                for ch, val in enumerate(vals):
+                    out[ch, pl.ds(pl.multiple_of(band * qrows, 8), qrows), lanes] = val
+
+            @pl.when((half == halves - 1) & (k < nd))
+            def _():
+                depth_copy(k, b, me_d).start()
+
+        keep_own(b)
 
         @pl.when(b > 0)
         def _():
             finish(b - 1)
+
+    @pl.loop(0, nb // 2)
+    def _(pair):
+        step(2 * pair, 0)
+        step(2 * pair + 1, 1)
 
     finish(nb - 1)
     if groups != nb:
@@ -345,9 +367,13 @@
     @pl.loop(0, nt)
     def _(o):
         for m in range(MOST):
-            label = arrived[o, 0, m]
-
-            @pl.when(label >= 0)
+            value = (2 * m - 1) * arrived[o, 0, m]
+            label = lax.rem(value, display.shape[2])
+            here = arrived[o, 0, m] != EMPTY
+            if m:
+                here = here & (value != -arrived[o, 0, 0])
+
+            @pl.when(here)
             def _():
                 for r in range(rpp):
                     piece = inbox[o, :, m * rpp + r:m * rpp + r + 1, :]
@@ -367,15 +393,12 @@
 
     order = jnp.arange(ppd, dtype=jnp.int32)
     owners = piece_home // ppd
-    shared = (owners[:, None] == owners[None, :]) & (order[None, :] < order[:, None])
-    earlier = jnp.sum(shared.astype(jnp.int32), axis=1)
-    target = ((owners - lax.axis_index("tile") + nt) % nt) * MOST + earlier
-    hit = jnp.arange(nt * MOST, dtype=jnp.int32)[:, None] == target[None, :]
-    route = jnp.sum(jnp.where(hit, order[None, :], 0), axis=1)
-    label = jnp.sum(jnp.where(hit, piece_home[None, :] % ppd + 1, 0), axis=1) - 1
-    labels = jnp.pad(label.reshape(nt, 1, MOST), ((0, 0), (0, 0), (0, 128 - MOST)))
-
-    ysend = jnp.stack([density[:, rows - 1], density[:, 0]])
+    code = order * ppd + piece_home % ppd
+    offset = (owners - lax.axis_index("tile") + nt) % nt
+    signs = jnp.where(jnp.arange(128) == 0, -1, 1)[None, None, :, None]
+    goes = offset[None, None, None, :] == jnp.arange(nt)[:, None, None, None]
+    codes = jnp.max(jnp.where(goes, signs * code[None, None, None, :], EMPTY), axis=3)
+    ylast, yfirst = density[:, rows - 1], density[:, 0]
     left, right = stencils(rows)
     anyspec = pl.BlockSpec(memory_space=pl.ANY)
     vmem = pl.BlockSpec(memory_space=pltpu.VMEM)
@@ -383,18 +406,20 @@
     dma = pltpu.SemaphoreType.DMA
     f32 = jnp.float32
     inbox, arrived = pl.pallas_call(
-        lambda *refs: brick_kernel(nd, nt, *refs),
+        lambda *refs: brick_kernel(nd, nt, ppd, *refs),
         out_shape=(jax.ShapeDtypeStruct((nt, 3, MOST * rpp, width), f32),
                    jax.ShapeDtypeStruct((nt, 1, 128), jnp.int32)),
-        in_specs=[smem, smem, anyspec, anyspec, anyspec, vmem, vmem],
+        in_specs=[smem, smem] + [anyspec] * 4 + [vmem] * 2,
         out_specs=(anyspec, anyspec),
         scratch_shapes=[
             pltpu.VMEM((cells + 2, rows, cols + 2 * PAD), jnp.bfloat16),
             pltpu.VMEM((2, cells, cols), jnp.bfloat16),
             pltpu.VMEM((2, cells, CB), f32),
-            pltpu.VMEM((2, cells, rows, CB), f32),
-            pltpu.VMEM((2, cells, rows, CB), f32),
-            pltpu.VMEM((5, RB, CB), f32),
+            pltpu.VMEM((cells, rows, CB), f32),
+            pltpu.VMEM((cells, rows, CB), f32),
+            pltpu.VMEM((cells, rows, CB), f32),
+            pltpu.VMEM((cells, rows, CB), f32),
+            pltpu.VMEM((5, qrows, CB), f32),
             pltpu.VMEM((4, rows, cols), f32),
             pltpu.VMEM((nd, 4, qrows, cols), f32),
             pltpu.VMEM((3, qrows, cols), f32),
@@ -404,7 +429,7 @@
         ],
         compiler_params=pltpu.CompilerParams(
             collective_id=0, has_side_effects=True, vmem_limit_bytes=56 * 1024 * 1024),
-    )(depth_rank, route, density, ysend, labels, left, right)
+    )(depth_rank, codes, density, ylast, yfirst, codes, left, right)
     return pl.pallas_call(
         place_kernel,
         out_shape=jax.ShapeDtypeStruct((3, 1, ppd, piece_len), f32),

time: 73.4 us -> 67.3 us (0.917)
  Pallas kernels: 68.2 us -> 62.8 us
  other arithmetic: 2.21 us -> 1.44 us
    pallas_call x1, Pallas kernels: 66 us -> 60.6 us  [on_device(): pl.pallas_call(lambda *refs: brick_kernel(nd, nt, ppd, *refs), out_shape=...]
    squeeze x0 -> x1, local copies, waits for them, and re-layouts: none -> 0.84 us  [on_device(): ylast, yfirst = (density[:, rows - 1], density[:, 0])]
    reduce_sum x2 -> x0, other arithmetic: 0.8 us -> none  [the longest x1 0.62 us: on_device(): jnp.sum(jnp.where(hit, piece_home[None, :] % ppd + 1, 0), axis=1) - 1]
where the time goes in v3:
time: 67.3 us; the launch traced here: 67.1 us
  Pallas kernels  62.8 us (93%)
  local copies, waits for them, and re-layouts  2.82 us (4%)
  other arithmetic  1.44 us (2%)
    pallas_call x1, Pallas kernels, on_device(): pl.pallas_call(lambda *refs: brick_kernel(nd, nt, ppd, *refs), out_shape=...  60.6 us
    pallas_call x1, Pallas kernels, on_device(): pl.pallas_call(place_kernel, out_shape=jax.ShapeDtypeStruct((3, 1, ppd, p...  2.15 us
    slice x1, local copies, waits for them, and re-layouts, on_device(): ylast, yfirst = (density[:, rows - 1], density[:, 0])  1.97 us

profile of v3, /device:TPU:0, one launch (start us, length us, event | category | flops | bytes accessed | tf_op | source)
XLA Modules:
  0.0 67.1 jit_solution(10684888701375588054)
XLA Ops:
  0.0 0.7 %and_select_fusion.1 = (s32[8]{0:T(128)S(1)}, s32[8]{0:T(128)S(1)}) fusion(s32[8]{0:T(128)} %param.7, s32[]{:T(128)S(6)} %axis_index.12), kind=kLoop, calls=%fused_computation.9 | loop fusion | flops 272 | bytes 100 | tf_op jit(solution)/shard_map/jit(remainder)/select_n | solution.py:397
  0.7 0.1 broadcast_multiply_fusion
  0.8 0.7 %select_reduce_fusion = s32[8,128]{1,0:T(8,128)} fusion(s32[128,8]{0,1:T(8,128)S(1)} %broadcast_multiply_fusion, pred[8,8]{1,0:T(8,128)(4,1)S(1)} %iota_compare_fusion), kind=kLoop, calls=%fused_computation.2 | loop fusion | flops 15360 | bytes 8256 | tf_op jit(solution)/shard_map/reduce_max | solution.py:400
  1.4 2.0 %fusion.2 = (bf16[32,1,2048]{2,1,0:T(2,128)(2,1)S(1)}, bf16[32,1,2048]{2,1,0:T(2,128)(2,1)S(1)}) fusion(bf16[32,64,2048]{2,1,0:T(8,128)(2,1)} %refs_2_.1), kind=kLoop, calls=%fused_computation.16 | loop fusion | bytes 524288 | tf_op jit(solution)/shard_map/slice | solution.py:401
  3.4 0.8 %copy_bitcast_fusion = (bf16[32,2048]{1,0:T(8,128)(2,1)}, bf16[32,2048]{1,0:T(8,128)(2,1)}) fusion(bf16[32,1,2048]{2,1,0:T(2,128)(2,1)S(1)} %get-tuple-element.9, bf16[32,1,2048]{2,1,0:T(2,128)(2,1)S(1)} %get-tuple-element.10), kind=kLoop, calls=%fused_computation | loop fusion | bytes 524288 | tf_op jit(solution)/shard_map/squeeze | solution.py:401
  4.3 60.6 %shard_map.55 = (f32[8,3,4,2048]{3,2,1,0:T(4,128)}, s32[8,1,128]{2,1,0:T(1,128)}) custom-call(s32[4]{0:T(128)} %refs_0_.1, s32[8,1,128]{2,1,0:T(1,128)} %bitcast.5, bf16[32,64,2048]{2,1,0:T(8,128)(2,1)} %refs_2_.1, bf16[32,2048]{1,0:T(8,128)(2,1)} %get-tuple-element.14.refs_3_, bf16[32,2048]{1,0:T(8,128)(2,1)} %get-tuple-element.13.refs_4_, ...), custom_call_target="tpu_custom_call" | custom-call | tf_op jit(solution)/shard_map/pallas_call | solution.py:408
  64.9 2.2 %shard_map.56 = f32[3,1,8,4096]{3,2,1,0:T(8,128)} custom-call(s32[8,1,128]{2,1,0:T(1,128)} %get-tuple-element.7.arrived, f32[8,3,4,2048]{3,2,1,0:T(4,128)} %get-tuple-element.8.inbox), custom_call_target="tpu_custom_call" | custom-call | tf_op jit(solution)/shard_map/pallas_call | solution.py:433
  (2 shorter events, 0.0 us)
